TPU v7x, 512 devices: a whole 4x4x16 slice. The times are simulated.
512 devices in a mesh: fsdp: 16 (over z_lo, core), tp: 32 (over x, y, z_hi).
Axes of the slice: x: 4, y: 4, z: 16 (z_hi: 2, z_lo: 8; z = z_hi * 8 + z_lo), core: 2. Of those that a mesh axis runs over, the one named last changes fastest.
Arguments:
- inputs: bfloat16 [128, 16, 8192], P('tp', None, 'fsdp'), may hold values from -6 to 6
- featurizer: bfloat16 [8192, 3, 8192], P('fsdp', None, 'tp'), may hold values from -0.0625 to 0.0625
- short_filter: float32 [3, 3, 8192], P(None, None, 'tp'), may hold values from -3 to 3
- long_filter: float32 [512, 128], P('tp'), may hold values from -1.2 to 1.2
- decay_rate: float32 [512], P('tp'), may hold values from 0.004 to 0.08
- skip_gain: float32 [8192], P('tp'), may hold values from -1 to 1
- output_grad: bfloat16 [128, 16, 8192], P(None, 'fsdp', 'tp'), may hold values from -6 to 6
Outputs:
- hyena_out: bfloat16 [128, 16, 8192], P(None, 'fsdp', 'tp')
- input_grad: bfloat16 [128, 16, 8192], P('tp', None, 'fsdp')
- weight_grad: bfloat16 [8192, 3, 8192], P('fsdp', None, 'tp')
All inputs are finite; a program needn't handle non-finite values.
Results may differ from a plain program's by a relative error of at most 0.028.
Values may be sent and summed in bfloat16 or wider, within the bound.
No kernel may reach another device: no remote copies, remote signals or barrier semaphores. Data moves between devices by JAX's collectives and lax.ppermute only.
A program may use at most 64 MiB of HBM per device.

v0:
```python
import jax
import jax.numpy as jnp
from jax import lax
from jax.sharding import PartitionSpec as P


def from_behind(x, axis, by):
    devices = lax.axis_size(axis)
    pairs = [(i, i + by) for i in range(devices) if 0 <= i + by < devices]
    return lax.ppermute(x, axis, pairs)


def toeplitz_pair(kernel, tokens):
    tap_count = kernel.shape[1]
    positions = jnp.arange(tokens)
    lag_grid = positions[:, None] - positions[None, :]
    near_inside = (lag_grid >= 0) & (lag_grid < tap_count)
    near_taken = jnp.take(kernel, jnp.clip(lag_grid, 0, tap_count - 1), axis=1)
    near_matrix = jnp.where(near_inside[None], near_taken, jnp.zeros_like(near_taken))
    far_grid = lag_grid + tokens
    far_inside = far_grid < tap_count
    far_taken = jnp.take(kernel, jnp.clip(far_grid, 0, tap_count - 1), axis=1)
    far_matrix = jnp.where(far_inside[None], far_taken, jnp.zeros_like(far_taken))
    return (near_matrix, far_matrix)


def add_sources(pieces):
    return tuple((jnp.sum(member, axis=1) for member in pieces))


def shards(inputs, featurizer, short_filter, long_filter, decay_rate, skip_gain, output_grad):
    gathered = lax.all_gather(inputs, "tp", axis=0, tiled=True)
    tokens, blocks, block_rows = gathered.shape
    halo_rows = short_filter.shape[0] - 1
    channels = featurizer.shape[2]
    wide_columns = 3 * channels
    border = jnp.zeros((halo_rows, 1, block_rows), gathered.dtype)
    earlier_rows = jnp.concatenate([border, gathered[tokens - halo_rows :, : blocks - 1]], axis=1)
    extended = jnp.concatenate([earlier_rows, gathered], axis=0)
    flat_ext = extended.reshape((tokens + halo_rows) * blocks, block_rows)
    partials = [
        jnp.dot(flat_ext, featurizer[:, stream, :], preferred_element_type=jnp.float32).reshape(
            tokens + halo_rows, blocks, channels
        )
        for stream in range(3)
    ]
    summed = add_sources(
        (
            lax.all_to_all(
                partials[0].astype(jnp.bfloat16), "fsdp", split_axis=1, concat_axis=1, tiled=True
            ).astype(jnp.float32),
            lax.all_to_all(
                partials[1].astype(jnp.bfloat16), "fsdp", split_axis=1, concat_axis=1, tiled=True
            ).astype(jnp.float32),
            lax.all_to_all(
                partials[2].astype(jnp.bfloat16), "fsdp", split_axis=1, concat_axis=1, tiled=True
            ).astype(jnp.float32),
        )
    )
    features = jnp.stack([member.astype(jnp.bfloat16) for member in summed], axis=1)
    feat_wide = features.astype(jnp.float32)
    filtered = short_filter[0] * feat_wide[halo_rows:]
    for lag_step in range(1, halo_rows + 1):
        filtered = (
            filtered
            + short_filter[lag_step]
            * feat_wide[halo_rows - lag_step : halo_rows - lag_step + tokens]
        )
    queries = filtered[:, 0]
    key_part = filtered[:, 1]
    value_part = filtered[:, 2]
    product = key_part * value_part
    offsets = jnp.arange(long_filter.shape[1]).astype(jnp.float32)
    kernel = long_filter * jnp.exp(-decay_rate[:, None] * offsets[None, :])
    near_matrix, far_matrix = toeplitz_pair(kernel, tokens)
    filter_count = kernel.shape[0]
    group_width = channels // filter_count
    grouped = product.reshape(tokens, filter_count, group_width)
    local_conv = jnp.einsum(
        "nst,tnc->snc", near_matrix, grouped, precision=lax.Precision.HIGHEST
    ).reshape(tokens, channels)
    earlier = from_behind(product.astype(jnp.bfloat16), "fsdp", 1).astype(product.dtype)
    far_conv = jnp.einsum(
        "nst,tnc->snc",
        far_matrix,
        earlier.reshape(tokens, filter_count, group_width),
        precision=lax.Precision.HIGHEST,
    ).reshape(tokens, channels)
    convolved = local_conv + far_conv + skip_gain * product
    hyena_out = (queries * convolved).astype(jnp.bfloat16).reshape(tokens, 1, channels)
    upstream = output_grad.reshape(tokens, channels).astype(jnp.float32)
    query_grad = upstream * convolved
    conv_grad = upstream * queries
    conv_grouped = conv_grad.reshape(tokens, filter_count, group_width)
    local_back = jnp.einsum(
        "nst,snc->tnc", near_matrix, conv_grouped, precision=lax.Precision.HIGHEST
    ).reshape(tokens, channels)
    later_grad = from_behind(conv_grad.astype(jnp.bfloat16), "fsdp", -1).astype(conv_grad.dtype)
    far_back = jnp.einsum(
        "nst,snc->tnc",
        far_matrix,
        later_grad.reshape(tokens, filter_count, group_width),
        precision=lax.Precision.HIGHEST,
    ).reshape(tokens, channels)
    product_grad = local_back + far_back + skip_gain * conv_grad
    filtered_grad = jnp.stack(
        [query_grad, product_grad * value_part, product_grad * key_part], axis=1
    )
    next_head = from_behind(filtered_grad[:halo_rows], "fsdp", -1)
    padded = jnp.concatenate([filtered_grad, next_head], axis=0)
    feature_grad = short_filter[0] * filtered_grad
    for lag_step in range(1, halo_rows + 1):
        feature_grad = feature_grad + short_filter[lag_step] * padded[lag_step : lag_step + tokens]
    grad_own = feature_grad.astype(jnp.bfloat16).reshape(tokens, 1, wide_columns)
    grad_all = lax.all_gather(grad_own, "fsdp", axis=1, tiled=True)
    weight_block = featurizer.reshape(block_rows, wide_columns)
    weight_grad = lax.dot_general(
        gathered, grad_all, (((0, 1), (0, 1)), ((), ())), preferred_element_type=jnp.float32
    )
    weight_grad = weight_grad.astype(jnp.bfloat16).reshape(featurizer.shape)
    own_count = tokens // lax.axis_size("tp")
    flat_piece = grad_all.reshape(own_count * lax.axis_size("tp") * blocks, wide_columns)
    result = lax.dot_general(
        flat_piece, weight_block, (((1,), (1,)), ((), ())), preferred_element_type=jnp.float32
    )
    input_grad = lax.psum_scatter(
        result.reshape(own_count * lax.axis_size("tp"), blocks, block_rows).astype(jnp.bfloat16),
        "tp",
        scatter_dimension=0,
        tiled=True,
    )
    return (hyena_out, input_grad, weight_grad)


def solution(mesh):
    in_specs = (
        P("tp", None, "fsdp"),
        P("fsdp", None, "tp"),
        P(None, None, "tp"),
        P("tp", None),
        P("tp"),
        P("tp"),
        P(None, "fsdp", "tp"),
    )
    out_specs = (P(None, "fsdp", "tp"), P("tp", None, "fsdp"), P("fsdp", None, "tp"))
    return jax.shard_map(shards, mesh=mesh, in_specs=in_specs, out_specs=out_specs, check_vma=False)
```

profile of v0, /device:TPU:4, one launch (start us, length us, event | category | flops | bytes accessed | tf_op | source)
XLA Modules:
  0.0 920.4 jit_solution(7407251781027713006)
XLA Ops:
  7.9 139.1 %all-gather.3.cloned.1.call-done = bf16[128,16,512]{2,1,0:T(8,128)(2,1)} async-done(((bf16[4,16,512]{2,1,0:T(8,128)(2,1)}), bf16[128,16,512]{2,1,0:T(8,128)(2,1)}) %all-gather.3.cloned.1.call-update) | async-done | bytes 2097168 | tf_op jit(solution)/shard_map/all_gather | solution.py:32
  147.8 2.3 convolution_convert_fusion.3
  150.1 1.4 copy.59
  151.4 3.7 all-to-all-start
  155.2 2.3 convolution_convert_fusion.2
  157.5 1.4 copy.61
  158.9 42.5 %all-to-all-done = bf16[130,16,256]{2,0,1:T(8,128)(2,1)S(1)} async-done(((bf16[130,16,256]{2,0,1:T(8,128)(2,1)}), bf16[130,16,256]{2,0,1:T(8,128)(2,1)S(1)}, u32[]{:S(2)}, u32[]{:S(2)}) %all-to-all-start) | async-done | bytes 1064992 | tf_op jit(solution)/shard_map/all_to_all | solution.py:49
  201.3 11.8 %all-to-all-start.1 = ((bf16[130,16,256]{2,0,1:T(8,128)(2,1)}), bf16[130,16,256]{2,0,1:T(8,128)(2,1)S(1)}, u32[]{:S(2)}, u32[]{:S(2)}) async-start(bf16[130,16,256]{2,0,1:T(8,128)(2,1)} %copy.61), calls=%async_computation.1 | async-start | bytes 2228224 | tf_op jit(solution)/shard_map/all_to_all | solution.py:52
  213.1 2.3 convolution_convert_fusion.1
  215.4 1.4 copy.63
  216.8 42.5 %all-to-all-done.1 = bf16[130,16,256]{2,0,1:T(8,128)(2,1)S(1)} async-done(((bf16[130,16,256]{2,0,1:T(8,128)(2,1)}), bf16[130,16,256]{2,0,1:T(8,128)(2,1)S(1)}, u32[]{:S(2)}, u32[]{:S(2)}) %all-to-all-start.1) | async-done | bytes 1064992 | tf_op jit(solution)/shard_map/all_to_all | solution.py:52
  259.3 11.8 %all-to-all-start.2 = ((bf16[130,16,256]{2,0,1:T(8,128)(2,1)}), bf16[130,16,256]{2,0,1:T(8,128)(2,1)}, u32[]{:S(2)}, u32[]{:S(2)}) async-start(bf16[130,16,256]{2,0,1:T(8,128)(2,1)} %copy.63), calls=%async_computation.2 | async-start | bytes 2228224 | tf_op jit(solution)/shard_map/all_to_all | solution.py:55
  271.4 54.8 %gather_fusion = f32[16384,16]{1,0:T(8,128)} fusion(f32[16,128]{0,1:T(8,128)S(1)} %copy.66, s32[16384]{0:T(1024)S(1)} %bitcast_clamp_fusion.1), kind=kCustom, calls=%fused_computation.clone | custom fusion | bytes 2162688 | tf_op jit(solution)/shard_map/jit(_take)/gather | solution.py:18
  326.2 5.2 copy.67
  331.5 54.8 %gather_fusion.1 = f32[16384,16]{1,0:T(8,128)} fusion(f32[16,128]{0,1:T(8,128)S(1)} %copy.66, s32[16384]{0:T(1024)S(1)} %bitcast_clamp_fusion), kind=kCustom, calls=%fused_computation.1.clone | custom fusion | bytes 2162688 | tf_op jit(solution)/shard_map/jit(_take)/gather | solution.py:22
  386.3 5.2 copy.70
  391.8 1.4 reduce_sum.37
  393.3 1.4 reduce_sum.38
  395.0 2.3 collective-permute-start
  397.4 1.7 fusion.7
  399.1 1.0 fusion.6
  400.2 1.4 collective-permute-start.1
  401.7 1.0 convolution_add_fusion.1
  402.8 1.8 collective-permute-done.1
  406.2 1.4 collective-permute-start.2
  407.7 4.2 collective-permute-done.2
  413.6 102.8 %all-gather.5.cloned.1.call-done = bf16[128,16,768]{2,0,1:T(8,128)(2,1)} async-done(((bf16[128,1,768]{2,0,1:T(8,128)(2,1)}), bf16[128,16,768]{2,0,1:T(8,128)(2,1)}) %all-gather.5.cloned.1.call-update) | async-done | bytes 3145744 | tf_op jit(solution)/shard_map/all_gather | solution.py:115
  516.4 3.7 convolution_convert_fusion
  520.1 2.5 copy.79
  522.7 5.3 bitcast_convert_fusion
  528.0 1.2 copy.82
  529.2 384.7 %reduce-scatter.2.cloned.1.call-done = bf16[4,16,512]{2,1,0:T(8,128)(2,1)} async-done(((bf16[128,16,512]{2,1,0:T(8,128)(2,1)}), bf16[4,16,512]{2,1,0:T(8,128)(2,1)}) %reduce-scatter.2.cloned.1.call-update) | async-done | bytes 65552 | tf_op jit(solution)/shard_map/reduce_scatter | solution.py:126
  (55 shorter events, 6.0 us)
Async XLA Ops:
  7.2 139.8 %all-gather.3.cloned.1.call-start = ((), (), s32[]{:S(2)}) async-start(), calls=%async_computation.4 | async-start | bytes 2162688 | tf_op jit(solution)/shard_map/all_gather | solution.py:32
  150.1 5.1 copy-start.1
  151.4 49.9 %all-to-all-start = ((bf16[130,16,256]{2,0,1:T(8,128)(2,1)}), bf16[130,16,256]{2,0,1:T(8,128)(2,1)S(1)}, u32[]{:S(2)}, u32[]{:S(2)}) async-start(bf16[130,16,256]{2,0,1:T(8,128)(2,1)} %copy.59), calls=%async_computation | async-start | bytes 2228224 | tf_op jit(solution)/shard_map/all_to_all | solution.py:49
  201.3 58.0 %all-to-all-start.1 = ((bf16[130,16,256]{2,0,1:T(8,128)(2,1)}), bf16[130,16,256]{2,0,1:T(8,128)(2,1)S(1)}, u32[]{:S(2)}, u32[]{:S(2)}) async-start(bf16[130,16,256]{2,0,1:T(8,128)(2,1)} %copy.61), calls=%async_computation.1 | async-start | bytes 2228224 | tf_op jit(solution)/shard_map/all_to_all | solution.py:52
  215.4 55.7 %copy-start.8 = (f32[16]{0:T(128)S(1)}, f32[16]{0:T(128)}, u32[]{:S(2)}) copy-start(f32[16]{0:T(128)} %param.13) | copy-start | bytes 196
  215.4 55.8 %copy-start.5 = (f32[16,128]{1,0:T(8,128)S(1)}, f32[16,128]{1,0:T(8,128)}, u32[]{:S(2)}) copy-start(f32[16,128]{1,0:T(8,128)} %param.12) | copy-start | bytes 24580
  259.3 11.9 %copy-start = (bf16[130,16,256]{2,0,1:T(8,128)(2,1)}, bf16[130,16,256]{2,0,1:T(8,128)(2,1)S(1)}, u32[]{:S(2)}) copy-start(bf16[130,16,256]{2,0,1:T(8,128)(2,1)S(1)} %all-to-all-done.1) | copy-start | bytes 3194884
  259.3 134.0 %all-to-all-start.2 = ((bf16[130,16,256]{2,0,1:T(8,128)(2,1)}), bf16[130,16,256]{2,0,1:T(8,128)(2,1)}, u32[]{:S(2)}, u32[]{:S(2)}) async-start(bf16[130,16,256]{2,0,1:T(8,128)(2,1)} %copy.63), calls=%async_computation.2 | async-start | bytes 2228224 | tf_op jit(solution)/shard_map/all_to_all | solution.py:55
  271.1 245.4 %all-gather.5.cloned.1.call-start = ((), (), s32[]{:S(2)}) async-start(), calls=%async_computation.5 | async-start | bytes 3342336 | tf_op jit(solution)/shard_map/all_gather | solution.py:115
  386.3 5.3 copy-start.4
  391.8 3.0 copy-start.3
  395.0 6.6 collective-permute-start
  400.2 5.3 copy-start.6
  400.2 4.4 collective-permute-start.1
  406.2 7.1 copy-start.2
  406.2 5.6 collective-permute-start.2
  413.1 500.8 %reduce-scatter.2.cloned.1.call-start = ((), (), s32[]{:S(2)}) async-start(), calls=%async_computation.6 | async-start | bytes 2162688 | tf_op jit(solution)/shard_map/reduce_scatter | solution.py:126
  520.1 2.6 copy-start.7
Sparse Core Ops, SparseCore 0:
  12.3 134.6 all-gather.2
  413.2 103.1 all-gather.4
  522.8 391.0 reduce-scatter.1
where the time goes:
time: 921 us; the launch traced here: 920 us
  waiting for transfers between devices  718 us (78%)
  local copies, waits for them, and re-layouts  131 us (14%)
  starting transfers between devices  32.6 us (4%)
  matrix products  20.3 us (2%)
  between operations  14.1 us (2%)
    reduce_scatter x1, waiting for transfers between devices, shards(): lax.psum_scatter(result.reshape(own_count * lax.axis_size('tp'), blocks,...  385 us
    all_gather x1, waiting for transfers between devices, shards(): gathered = lax.all_gather(inputs, 'tp', axis=0, tiled=True)  139 us
    all_gather x1, waiting for transfers between devices, shards(): grad_all = lax.all_gather(grad_own, 'fsdp', axis=1, tiled=True)  103 us
    gather x2, local copies, waits for them, and re-layouts, toeplitz_pair(): far_taken = jnp.take(kernel, jnp.clip(far_grid, 0, tap_count - 1), axis=1)  60 us
    gather x2, local copies, waits for them, and re-layouts, toeplitz_pair(): near_taken = jnp.take(kernel, jnp.clip(lag_grid, 0, tap_count - 1), axis=1)  60 us
    all_to_all x1, waiting for transfers between devices, shards(): lax.all_to_all(partials[1].astype(jnp.bfloat16), 'fsdp', split_axis=1, co...  42.5 us
    all_to_all x1, waiting for transfers between devices, shards(): lax.all_to_all(partials[0].astype(jnp.bfloat16), 'fsdp', split_axis=1, co...  42.5 us
  transfers between devices with their start and end apart: 9, of which 7 were waited for; matrix products, arithmetic and copies ran while one was open for 15% of the time, Pallas kernels for 0%

commit v1 on v0

--- a/solution.py
+++ b/solution.py
@@ -112,7 +112,9 @@
     for lag_step in range(1, halo_rows + 1):
         feature_grad = feature_grad + short_filter[lag_step] * padded[lag_step : lag_step + tokens]
     grad_own = feature_grad.astype(jnp.bfloat16).reshape(tokens, 1, wide_columns)
-    grad_all = lax.all_gather(grad_own, "fsdp", axis=1, tiled=True)
+    grad_all = jnp.concatenate(
+        lax.all_to_all(jnp.stack([grad_own] * lax.axis_size("fsdp")), "fsdp", 0, 0), axis=1
+    )
     weight_block = featurizer.reshape(block_rows, wide_columns)
     weight_grad = lax.dot_general(
         gathered, grad_all, (((0, 1), (0, 1)), ((), ())), preferred_element_type=jnp.float32

time: 921 us -> 975 us (1.059)
  the two profiles are of different devices: /device:TPU:4 before, /device:TPU:32 now
where the time goes in v1:
time: 975 us; the launch traced here: 974 us
  waiting for transfers between devices  747 us (77%)
  local copies, waits for them, and re-layouts  134 us (14%)
  starting transfers between devices  53.3 us (5%)
  matrix products  20.2 us (2%)
  between operations  14.4 us (1%)
    reduce_scatter x1, waiting for transfers between devices, shards(): lax.psum_scatter(result.reshape(own_count * lax.axis_size('tp'), blocks,...  396 us
    all_gather x1, waiting for transfers between devices, shards(): gathered = lax.all_gather(inputs, 'tp', axis=0, tiled=True)  134 us
    all_to_all x1, waiting for transfers between devices, shards(): lax.all_to_all(jnp.stack([grad_own] * lax.axis_size('fsdp')), 'fsdp', 0, 0)  129 us
    gather x2, local copies, waits for them, and re-layouts, toeplitz_pair(): far_taken = jnp.take(kernel, jnp.clip(far_grid, 0, tap_count - 1), axis=1)  59.7 us
    gather x2, local copies, waits for them, and re-layouts, toeplitz_pair(): near_taken = jnp.take(kernel, jnp.clip(lag_grid, 0, tap_count - 1), axis=1)  59.7 us
    all_to_all x1, waiting for transfers between devices, shards(): lax.all_to_all(partials[0].astype(jnp.bfloat16), 'fsdp', split_axis=1, co...  42.7 us
    all_to_all x1, waiting for transfers between devices, shards(): lax.all_to_all(partials[1].astype(jnp.bfloat16), 'fsdp', split_axis=1, co...  42.6 us
  transfers between devices with their start and end apart: 9, of which 7 were waited for; matrix products, arithmetic and copies ran while one was open for 15% of the time, Pallas kernels for 0%

profile of v1, /device:TPU:32, one launch (start us, length us, event | category | flops | bytes accessed | tf_op | source)
XLA Modules:
  0.0 973.8 jit_solution(2551921548365953898)
XLA Ops:
  7.9 134.1 %all-gather.2.cloned.1.call-done = bf16[128,16,512]{2,1,0:T(8,128)(2,1)} async-done(((bf16[4,16,512]{2,1,0:T(8,128)(2,1)}), bf16[128,16,512]{2,1,0:T(8,128)(2,1)}) %all-gather.2.cloned.1.call-update) | async-done | bytes 2097168 | tf_op jit(solution)/shard_map/all_gather | solution.py:32
  142.7 2.3 convolution_convert_fusion.2
  145.0 1.4 copy.59
  146.4 10.2 %all-to-all-start = ((bf16[130,16,256]{2,0,1:T(8,128)(2,1)}), bf16[130,16,256]{2,0,1:T(8,128)(2,1)S(1)}, u32[]{:S(2)}, u32[]{:S(2)}) async-start(bf16[130,16,256]{2,0,1:T(8,128)(2,1)} %copy.59), calls=%async_computation | async-start | bytes 2228224 | tf_op jit(solution)/shard_map/all_to_all | solution.py:49
  156.6 2.3 convolution_convert_fusion.1
  158.9 1.4 copy.61
  160.3 42.7 %all-to-all-done = bf16[130,16,256]{2,0,1:T(8,128)(2,1)S(1)} async-done(((bf16[130,16,256]{2,0,1:T(8,128)(2,1)}), bf16[130,16,256]{2,0,1:T(8,128)(2,1)S(1)}, u32[]{:S(2)}, u32[]{:S(2)}) %all-to-all-start) | async-done | bytes 1064992 | tf_op jit(solution)/shard_map/all_to_all | solution.py:49
  203.0 11.6 %all-to-all-start.1 = ((bf16[130,16,256]{2,0,1:T(8,128)(2,1)}), bf16[130,16,256]{2,0,1:T(8,128)(2,1)S(1)}, u32[]{:S(2)}, u32[]{:S(2)}) async-start(bf16[130,16,256]{2,0,1:T(8,128)(2,1)} %copy.61), calls=%async_computation.1 | async-start | bytes 2228224 | tf_op jit(solution)/shard_map/all_to_all | solution.py:52
  214.7 2.3 convolution_convert_fusion
  217.0 1.4 copy.63
  218.4 42.6 %all-to-all-done.1 = bf16[130,16,256]{2,0,1:T(8,128)(2,1)S(1)} async-done(((bf16[130,16,256]{2,0,1:T(8,128)(2,1)}), bf16[130,16,256]{2,0,1:T(8,128)(2,1)S(1)}, u32[]{:S(2)}, u32[]{:S(2)}) %all-to-all-start.1) | async-done | bytes 1064992 | tf_op jit(solution)/shard_map/all_to_all | solution.py:52
  261.0 11.6 %all-to-all-start.2 = ((bf16[130,16,256]{2,0,1:T(8,128)(2,1)}), bf16[130,16,256]{2,0,1:T(8,128)(2,1)}, u32[]{:S(2)}, u32[]{:S(2)}) async-start(bf16[130,16,256]{2,0,1:T(8,128)(2,1)} %copy.63), calls=%async_computation.2 | async-start | bytes 2228224 | tf_op jit(solution)/shard_map/all_to_all | solution.py:55
  272.9 54.5 %gather_fusion = f32[16384,16]{1,0:T(8,128)} fusion(f32[16,128]{0,1:T(8,128)S(1)} %copy.66, s32[16384]{0:T(1024)S(1)} %bitcast_clamp_fusion.1), kind=kCustom, calls=%fused_computation.clone | custom fusion | bytes 2162688 | tf_op jit(solution)/shard_map/jit(_take)/gather | solution.py:18
  327.4 5.2 copy.67
  332.6 54.5 %gather_fusion.1 = f32[16384,16]{1,0:T(8,128)} fusion(f32[16,128]{0,1:T(8,128)S(1)} %copy.66, s32[16384]{0:T(1024)S(1)} %bitcast_clamp_fusion), kind=kCustom, calls=%fused_computation.1.clone | custom fusion | bytes 2162688 | tf_op jit(solution)/shard_map/jit(_take)/gather | solution.py:22
  387.2 5.2 copy.70
  392.7 1.4 reduce_sum.37
  394.1 1.4 reduce_sum.38
  395.9 2.0 collective-permute-start
  398.0 1.7 fusion.15
  400.8 3.7 collective-permute-start.1
  408.0 3.7 collective-permute-start.2
  411.7 1.3 collective-permute-done.2
  413.5 2.0 stack.26
  415.5 10.2 %all-to-all-start.3 = ((bf16[16,128,1,768]{3,1,2,0:T(8,128)(2,1)}), bf16[16,128,1,768]{3,1,2,0:T(8,128)(2,1)S(1)}, u32[]{:S(2)}, u32[]{:S(2)}) async-start(bf16[16,128,1,768]{3,1,2,0:T(8,128)(2,1)} %stack.26), calls=%async_computation.3 | async-start | bytes 6291456 | tf_op jit(solution)/shard_map/all_to_all | solution.py:116
  425.9 2.3 copy.78
  428.2 129.1 %all-to-all-done.3 = bf16[16,128,1,768]{3,1,2,0:T(8,128)(2,1)S(1)} async-done(((bf16[16,128,1,768]{3,1,2,0:T(8,128)(2,1)}), bf16[16,128,1,768]{3,1,2,0:T(8,128)(2,1)S(1)}, u32[]{:S(2)}, u32[]{:S(2)}) %all-to-all-start.3) | async-done | bytes 3145760 | tf_op jit(solution)/shard_map/all_to_all | solution.py:116
  557.3 2.9 fusion.7
  560.2 2.5 copy.80
  562.7 5.9 bitcast_convert_fusion
  568.6 2.3 copy.83
  570.9 396.1 %reduce-scatter.2.cloned.1.call-done = bf16[4,16,512]{2,1,0:T(8,128)(2,1)} async-done(((bf16[128,16,512]{2,1,0:T(8,128)(2,1)}), bf16[4,16,512]{2,1,0:T(8,128)(2,1)}) %reduce-scatter.2.cloned.1.call-update) | async-done | bytes 65552 | tf_op jit(solution)/shard_map/reduce_scatter | solution.py:128
  (51 shorter events, 7.7 us)
Async XLA Ops:
  7.2 134.8 %all-gather.2.cloned.1.call-start = ((), (), s32[]{:S(2)}) async-start(), calls=%async_computation.5 | async-start | bytes 2162688 | tf_op jit(solution)/shard_map/all_gather | solution.py:32
  145.0 11.6 %copy-start.1 = (bf16[512,3,256]{2,0,1:T(8,128)(2,1)S(1)}, bf16[512,3,256]{2,0,1:T(8,128)(2,1)}, u32[]{:S(2)}) copy-start(bf16[512,3,256]{2,0,1:T(8,128)(2,1)} %param.10) | copy-start | bytes 2359300
  146.4 56.6 %all-to-all-start = ((bf16[130,16,256]{2,0,1:T(8,128)(2,1)}), bf16[130,16,256]{2,0,1:T(8,128)(2,1)S(1)}, u32[]{:S(2)}, u32[]{:S(2)}) async-start(bf16[130,16,256]{2,0,1:T(8,128)(2,1)} %copy.59), calls=%async_computation | async-start | bytes 2228224 | tf_op jit(solution)/shard_map/all_to_all | solution.py:49
  203.0 58.0 %all-to-all-start.1 = ((bf16[130,16,256]{2,0,1:T(8,128)(2,1)}), bf16[130,16,256]{2,0,1:T(8,128)(2,1)S(1)}, u32[]{:S(2)}, u32[]{:S(2)}) async-start(bf16[130,16,256]{2,0,1:T(8,128)(2,1)} %copy.61), calls=%async_computation.1 | async-start | bytes 2228224 | tf_op jit(solution)/shard_map/all_to_all | solution.py:52
  217.0 55.6 %copy-start.6 = (f32[16]{0:T(128)S(1)}, f32[16]{0:T(128)}, u32[]{:S(2)}) copy-start(f32[16]{0:T(128)} %param.13) | copy-start | bytes 196
  217.0 55.7 %copy-start.4 = (f32[16,128]{1,0:T(8,128)S(1)}, f32[16,128]{1,0:T(8,128)}, u32[]{:S(2)}) copy-start(f32[16,128]{1,0:T(8,128)} %param.12) | copy-start | bytes 24580
  261.0 11.6 %copy-start = (bf16[130,16,256]{2,0,1:T(8,128)(2,1)}, bf16[130,16,256]{2,0,1:T(8,128)(2,1)S(1)}, u32[]{:S(2)}) copy-start(bf16[130,16,256]{2,0,1:T(8,128)(2,1)S(1)} %all-to-all-done.1) | copy-start | bytes 3194884
  261.0 133.1 %all-to-all-start.2 = ((bf16[130,16,256]{2,0,1:T(8,128)(2,1)}), bf16[130,16,256]{2,0,1:T(8,128)(2,1)}, u32[]{:S(2)}, u32[]{:S(2)}) async-start(bf16[130,16,256]{2,0,1:T(8,128)(2,1)} %copy.63), calls=%async_computation.2 | async-start | bytes 2228224 | tf_op jit(solution)/shard_map/all_to_all | solution.py:55
  387.2 5.3 copy-start.3
  392.7 3.0 copy-start.2
  395.9 8.6 collective-permute-start
  400.8 6.5 copy-start.5
  400.8 5.6 collective-permute-start.1
  408.0 5.0 collective-permute-start.2
  415.5 141.8 %all-to-all-start.3 = ((bf16[16,128,1,768]{3,1,2,0:T(8,128)(2,1)}), bf16[16,128,1,768]{3,1,2,0:T(8,128)(2,1)S(1)}, u32[]{:S(2)}, u32[]{:S(2)}) async-start(bf16[16,128,1,768]{3,1,2,0:T(8,128)(2,1)} %stack.26), calls=%async_computation.3 | async-start | bytes 6291456 | tf_op jit(solution)/shard_map/all_to_all | solution.py:116
  425.7 541.3 %reduce-scatter.2.cloned.1.call-start = ((), (), s32[]{:S(2)}) async-start(), calls=%async_computation.6 | async-start | bytes 2162688 | tf_op jit(solution)/shard_map/reduce_scatter | solution.py:128
Sparse Core Ops, SparseCore 0:
  12.3 129.6 all-gather.1
  562.9 404.0 reduce-scatter.1
